TPU v7x, 512 devices: a whole 4x4x16 slice. The times are simulated.
512 devices in a mesh: lat: 64 (over z, y), ord: 2 (over core), orb: 4 (over x).
Axes of the slice: x: 4, y: 4, z: 16, core: 2. Of those that a mesh axis runs over, the one named last changes fastest.
Arguments:
- anomaly: bfloat16 [2, 1024, 4320], P(None, 'lat'), may hold values from -6 to 6
- row_weight: float32 [2, 1024], replicated, may hold values from 0.2 to 1
- panel: bfloat16 [4, 64, 1024, 2, 640], P('orb', None, 'lat', 'ord'), may hold values from -0.125 to 0.125
- order_value: int32 [4, 64], P('orb'), may hold values from 0 to 2159
- deg_first: int32 [4, 64], P('orb', 'lat'), may hold values from 0 to 2190
- sat_rows: bfloat16 [131072, 256], P(('lat', 'ord', 'orb')), may hold values from -0.25 to 0.25
- sat_slot: int32 [131072, 1], P(('lat', 'ord', 'orb')), may hold values from 0 to 255; in each aligned block of 256 rows (0 to 255, 256 to 511, ...) at most 2 rows name the same one
Outputs:
- normals: float32 [4, 64, 2, 640, 2, 640], P('orb', 'lat', 'ord')
- right_side: float32 [4, 64, 2, 2, 640], P('orb', 'lat', None, 'ord')
Inputs may be any that keep to these rules, and one draw needn't show every extreme that they name: `sat_slot`: among the 256 rows of one device no order slot appears more than 2 times.
All inputs are finite; a program needn't handle non-finite values.
Results may differ from a plain program's by a relative error of at most 0.0029.
Values may be sent and summed in bfloat16 or wider, within the bound.
No kernel may reach another device: no remote copies, remote signals or barrier semaphores. Data moves between devices by JAX's collectives and lax.ppermute only.
A program may use at most 64 MiB of HBM per device.

v0:
```python
import math
import jax
import jax.numpy as jnp
from jax import lax
from jax.sharding import PartitionSpec as P

LMAX = 2190


def window_flags(first_degree, order_now, half_count):
    parity_col = (
        jnp.arange(2, dtype=jnp.int32)[:, None]
        + 2 * jnp.arange(half_count, dtype=jnp.int32)[None, :]
    )
    degree = first_degree[:, None, None] + parity_col[None]
    live_flags = (degree <= LMAX).astype(jnp.float32)
    parity = (degree + order_now[:, None, None]) % 2
    return (live_flags, 1.0 - 2.0 * parity.astype(jnp.float32))


def fourier_table(order_row, length):
    sample = jnp.arange(length, dtype=jnp.int32)
    phase_index = sample[:, None] * order_row[None, :] % length
    angle_value = phase_index.astype(jnp.float32) * (2.0 * math.pi / length)
    return jnp.concatenate([jnp.cos(angle_value), jnp.sin(angle_value)], axis=1)


def parity_gram(received):
    sat_width = received.shape[-1]
    sat_block = received.reshape(received.shape[0], -1, sat_width)
    split_block = sat_block.reshape(sat_block.shape[0], sat_block.shape[1], 2, sat_width // 2)
    return jnp.einsum("irpa,irl->pial", split_block, sat_block, preferred_element_type=jnp.float32)


def shards(anomaly, row_weight, panel, order_value, deg_first, sat_rows, sat_slot):
    lat_count = lax.axis_size("lat")
    orb_count = lax.axis_size("orb")
    lat_index = lax.axis_index("lat")
    parity_index = lax.axis_index("ord")
    group_orders = panel.shape[1]
    row_count = panel.shape[2]
    half_count = panel.shape[4]
    lon_count = anomaly.shape[2]
    trig_table = fourier_table(order_value[0], lon_count)
    spectra = jnp.einsum(
        "hrk,kc->hrc", anomaly.astype(jnp.float32), trig_table, precision=lax.Precision.HIGHEST
    ) * math.sqrt(2.0 / lon_count)
    local_weight = lax.dynamic_slice_in_dim(row_weight, lat_index * row_count, row_count, 1)
    north_terms = spectra[0] * local_weight[0][:, None]
    south_terms = spectra[1] * local_weight[1][:, None]
    coefficients = jnp.stack(
        [
            north_terms[:, :group_orders],
            north_terms[:, group_orders:],
            south_terms[:, :group_orders],
            south_terms[:, group_orders:],
        ],
        axis=-1,
    )
    coefficients = jnp.transpose(coefficients, (1, 0, 2))[None].astype(jnp.bfloat16)
    own_order = lax.dynamic_slice_in_dim(order_value[0], lat_index, 1, 0)
    live_pair, sign_pair = window_flags(deg_first[0], own_order, half_count)
    live_own = lax.dynamic_index_in_dim(live_pair[0], parity_index, 0, keepdims=False)
    sign_own = lax.dynamic_index_in_dim(sign_pair[0], parity_index, 0, keepdims=False)
    live_mask = live_own.astype(jnp.bfloat16)
    panel_piece = panel[0, :, :, 0, :]
    coef_piece = coefficients[0]
    summed = lax.psum_scatter(
        jnp.einsum("ori,orc->oci", panel_piece, coef_piece, preferred_element_type=jnp.float32),
        "lat",
        scatter_dimension=0,
        tiled=True,
    )
    products = summed[0] * live_own[None, :]
    arrived_panel = lax.all_to_all(panel, "lat", split_axis=1, concat_axis=2, tiled=True)
    masked_own = arrived_panel[0, 0, :, 0, :] * live_mask[None, :]
    right_cos = products[0] + sign_own * products[2]
    right_sin = products[1] + sign_own * products[3]
    right_side = jnp.stack([right_cos, right_sin], axis=0)[None, None, :, None, :]
    parity_pair = lax.all_gather(masked_own[:, None, :], "ord", axis=1, tiled=True)
    plus_weight = (row_weight[0] + row_weight[1])[:, None, None]
    minus_weight = (row_weight[0] - row_weight[1])[:, None, None]
    plus_panel = (parity_pair.astype(jnp.float32) * plus_weight).astype(jnp.bfloat16)
    minus_panel = (parity_pair.astype(jnp.float32) * minus_weight).astype(jnp.bfloat16)
    full_plus = jnp.einsum(
        "ri,rqj->iqj", masked_own, plus_panel, preferred_element_type=jnp.float32
    )
    full_minus = jnp.einsum(
        "ri,rqj->iqj", masked_own, minus_panel, preferred_element_type=jnp.float32
    )
    same_parity = (jnp.arange(2, dtype=jnp.int32) == parity_index)[None, :, None]
    grid_normal = jnp.where(same_parity, full_plus, full_minus)
    sat_order = sat_slot[:, 0]
    sat_count = sat_order.shape[0]
    sat_width = sat_rows.shape[1]
    half_sat = sat_width // 2
    orders_all = orb_count * group_orders
    slot_cap = max(2, 2 * sat_count // orders_all)
    position = jnp.arange(sat_count, dtype=jnp.int32)
    earlier = (sat_order[:, None] == sat_order[None, :]) & (position[None, :] < position[:, None])
    slot_rank = jnp.sum(earlier, axis=1, dtype=jnp.int32)
    group_id = sat_order // group_orders
    within = sat_order % group_orders
    destination = (group_id * lat_count + within) * slot_cap + slot_rank
    reordered = (
        sat_rows.reshape(sat_count, half_sat, 2).transpose(0, 2, 1).reshape(sat_count, sat_width)
    )
    buffer = (
        jnp.zeros((orb_count * lat_count * slot_cap, sat_width), jnp.bfloat16)
        .at[destination]
        .set(reordered)
    )
    buffer = buffer.reshape(orb_count, lat_count, slot_cap, sat_width)
    partial_value = parity_gram(
        lax.all_to_all(buffer, "lat", split_axis=1, concat_axis=1, tiled=True)
    )
    sat_half = lax.psum_scatter(
        partial_value.reshape(-1, sat_width), ("ord", "orb"), scatter_dimension=0, tiled=True
    )
    sat_block = sat_half.reshape(half_sat, 2, half_sat)
    padded = jnp.pad(sat_block, ((0, half_count - half_sat), (0, 0), (0, half_count - half_sat)))
    normals = grid_normal + padded * (live_own[:, None, None] * live_pair[0][None, :, :])
    return (normals[None, None, None], right_side)


def solution(mesh):
    in_specs = (
        P(None, "lat", None),
        P(),
        P("orb", None, "lat", "ord", None),
        P("orb", None),
        P("orb", "lat"),
        P(("lat", "ord", "orb"), None),
        P(("lat", "ord", "orb"), None),
    )
    out_specs = (P("orb", "lat", "ord", None, None, None), P("orb", "lat", None, "ord", None))
    return jax.shard_map(shards, mesh=mesh, in_specs=in_specs, out_specs=out_specs, check_vma=False)
```

profile of v0, /device:TPU:1, one launch (start us, length us, event | category | flops | bytes accessed | tf_op | source)
XLA Modules:
  0.0 386.9 jit_solution(14121209996420184971)
XLA Ops:
  8.0 0.0 copy-start
  8.0 0.9 convert_reduce_fusion
  8.9 0.7 compare_select_fusion.2
  9.6 1.0 copy.52
  10.7 0.1 reshape.237
  10.7 0.1 copy.54
  10.8 0.0 copy-start.1
  10.9 0.0 copy-start.2
  10.9 1.5 scatter_custom_fusion
  12.4 0.1 reshape.239
  12.5 0.2 copy.55
  12.7 38.5 %all_to_all.14 = bf16[4,64,2,256]{3,2,0,1:T(2,128)(2,1)S(1)} all-to-all(bf16[4,64,2,256]{3,2,0,1:T(2,128)(2,1)S(1)} %copy.55), channel_id=1, replica_groups=mesh['lat'=64,'ord'=2,'orb'=4] {'lat'}, dimensions={1} | all-to-all | bytes 524288 | tf_op jit(solution)/shard_map/all_to_all | solution.py:115
  51.3 7.0 %all-to-all-start = ((bf16[1,64,16,1,640]{4,2,3,0,1:T(8,128)(2,1)}), bf16[1,64,16,1,640]{4,2,3,0,1:T(8,128)(2,1)S(1)}, u32[]{:S(2)}, u32[]{:S(2)}) async-start(bf16[1,64,16,1,640]{4,2,3,0,1:T(8,128)(2,1)} %bitcast), calls=%async_computation | async-start | bytes 2621440 | tf_op jit(solution)/shard_map/all_to_all | solution.py:75
  58.3 0.2 all-reduce.4.cloned.1.call-start
  58.6 0.0 copy-done.1
  58.6 0.1 constant_dynamic-slice_fusion.1
  58.7 0.0 copy-done.2
  58.7 8.9 %fusion.16 = (f32[4320,64]{1,0:T(8,128)S(1)}, f32[4320,64]{1,0:T(8,128)S(1)}) fusion(s32[64]{0:T(128)S(1)} %bitcast.98), kind=kLoop, calls=%fused_computation.21 | loop fusion | flops 2488320 | bytes 2212096 | tf_op jit(solution)/shard_map/cos | solution.py:25
  67.6 0.0 copy-done
  67.6 1.2 fusion.27
  68.8 0.1 fusion.37
  68.9 0.1 slice_bitcast_fusion.3
  69.0 0.1 copy.62
  69.1 2.5 fusion.20
  71.6 0.0 all-reduce.4.cloned.1.call-update
  71.6 0.3 reduce-scatter.2.cloned.1.call-start
  71.9 0.2 copy.56
  72.1 0.2 reshape_reshape.3
  72.3 0.1 reshape.240
  72.4 0.2 copy.58
  72.6 0.3 fusion.48
  72.9 1.0 copy.59
  73.9 0.0 reduce-scatter.2.cloned.1.call-update
  73.9 0.0 all-gather.2.cloned.1.call-start
  74.0 0.6 constant_dynamic-slice_fusion
  75.2 0.7 compare_select_fusion
  75.9 46.8 %all-to-all-done = bf16[1,64,16,1,640]{4,2,3,0,1:T(8,128)(2,1)S(1)} async-done(((bf16[1,64,16,1,640]{4,2,3,0,1:T(8,128)(2,1)}), bf16[1,64,16,1,640]{4,2,3,0,1:T(8,128)(2,1)S(1)}, u32[]{:S(2)}, u32[]{:S(2)}) %all-to-all-start) | async-done | bytes 1310752 | tf_op jit(solution)/shard_map/all_to_all | solution.py:75
  122.8 1.2 broadcast_multiply_fusion
  123.9 0.0 all-gather.2.cloned.1.call-update
  124.0 1.3 dynamic-slice.3
  125.3 212.7 %all-reduce.4.cloned.1.call-done = f32[64,4,640]{2,1,0:T(4,128)} async-done(((f32[64,4,640]{2,1,0:T(4,128)}), f32[64,4,640]{2,1,0:T(4,128)}) %all-reduce.4.cloned.1.call-update) | async-done | bytes 655376
  338.0 1.4 fusion.33
  339.4 0.6 copy.64
  340.0 0.0 reduce-scatter.2.cloned.1.call-done
  340.0 1.0 copy.60
  341.0 0.1 copy.61
  341.1 0.7 copy.51
  341.7 27.3 %all-gather.2.cloned.1.call-done = bf16[1024,2,640]{2,0,1:T(8,128)(2,1)} async-done(((bf16[1024,1,640]{2,0,1:T(8,128)(2,1)}), bf16[1024,2,640]{2,0,1:T(8,128)(2,1)}) %all-gather.2.cloned.1.call-update) | async-done | bytes 2621456 | tf_op jit(solution)/shard_map/all_gather | solution.py:80
  369.1 0.0 copy-start.3
  369.1 3.9 %fusion.2 = f32[640,2,640]{2,0,1:T(8,128)S(1)} fusion(bf16[1024,2,640]{2,0,1:T(8,128)(2,1)} %all-gather.2.cloned.1.call-done, f32[1024]{0:T(1024)S(1)} %bitcast.96, bf16[1024,640]{0,1:T(8,128)(2,1)S(1)} %copy.51, bf16[640]{0:T(1024)(128)(2,1)S(1)} %convert_element_type.57), kind=kOutput, calls=%fused_computation.7 | convolution fusion | flops 1684275200 | bytes 7214336 | tf_op jit(solution)/shard_map/ri,rqj->iqj/dot_general | solution.py:88
  373.0 0.0 copy-done.3
  373.0 2.2 add_bitcast_fusion
  375.2 4.2 %copy.63 = f32[1,1,1,640,2,640]{5,4,3,2,1,0:T(2,128)} copy(f32[1,1,1,640,2,640]{5,3,4,2,1,0:T(8,128)S(1)} %add_bitcast_fusion) | data formatting | bytes 6553600
  (11 shorter events, 0.1 us)
Async XLA Ops:
  8.0 59.6 %copy-start = (bf16[2,16,4320]{2,1,0:T(8,128)(2,1)S(1)}, bf16[2,16,4320]{2,1,0:T(8,128)(2,1)}, u32[]{:S(2)}) copy-start(bf16[2,16,4320]{2,1,0:T(8,128)(2,1)} %param.7) | copy-start | bytes 829444
  10.8 47.7 %copy-start.1 = (f32[2,1024]{1,0:T(2,128)S(1)}, f32[2,1024]{1,0:T(2,128)}, u32[]{:S(2)}) copy-start(f32[2,1024]{1,0:T(2,128)} %param.8) | copy-start | bytes 24580
  10.9 47.8 %copy-start.2 = (s32[1,64]{1,0:T(1,128)S(1)}, s32[1,64]{1,0:T(1,128)}, u32[]{:S(2)}) copy-start(s32[1,64]{1,0:T(1,128)} %param.10) | copy-start | bytes 772
  51.3 71.5 %all-to-all-start = ((bf16[1,64,16,1,640]{4,2,3,0,1:T(8,128)(2,1)}), bf16[1,64,16,1,640]{4,2,3,0,1:T(8,128)(2,1)S(1)}, u32[]{:S(2)}, u32[]{:S(2)}) async-start(bf16[1,64,16,1,640]{4,2,3,0,1:T(8,128)(2,1)} %bitcast), calls=%async_computation | async-start | bytes 2621440 | tf_op jit(solution)/shard_map/all_to_all | solution.py:75
  58.3 279.6 %all-reduce.4.cloned.1.call-start = ((), (), s32[]{:S(2)}) async-start(), calls=%async_computation.5 | async-start | bytes 1310720
  71.6 268.3 %reduce-scatter.2.cloned.1.call-start = ((), (), s32[]{:S(2)}) async-start(), calls=%async_computation.4 | async-start | bytes 1179648 | tf_op jit(solution)/shard_map/reduce_scatter | solution.py:117
  73.9 295.1 %all-gather.2.cloned.1.call-start = ((), (), s32[]{:S(2)}) async-start(), calls=%async_computation.3 | async-start | bytes 3932160 | tf_op jit(solution)/shard_map/all_gather | solution.py:80
  369.1 3.9 %copy-start.3 = (bf16[1024,2,640]{2,0,1:T(8,128)(2,1)S(1)}, bf16[1024,2,640]{2,0,1:T(8,128)(2,1)}, u32[]{:S(2)}) copy-start(bf16[1024,2,640]{2,0,1:T(8,128)(2,1)} %all-gather.2.cloned.1.call-done) | copy-start | bytes 7864324
Sparse Core Ops, SparseCore 0:
  71.7 266.1 all-reduce.3
  340.6 28.3 all-gather.1
Sparse Core Ops, SparseCore 1:
  74.9 44.1 reduce-scatter.1
where the time goes:
time: 387 us
  waiting for transfers between devices  287 us (74%)
  blocking collectives  38.5 us (10%)
  between operations  16.4 us (4%)
  other arithmetic  13.9 us (4%)
  local copies, waits for them, and re-layouts  13.4 us (3%)
  matrix products  10.1 us (3%)
  starting transfers between devices  7.58 us (2%)
    unnamed x4, waiting for transfers between devices  213 us
    all_to_all x1, waiting for transfers between devices, shards(): lax.all_to_all(panel, 'lat', split_axis=1, concat_axis=2, tiled=True)  46.8 us
    all_to_all x1, blocking collectives, shards(): lax.all_to_all(buffer, 'lat', split_axis=1, concat_axis=1, tiled=True)  38.5 us
    all_gather x1, waiting for transfers between devices, shards(): lax.all_gather(masked_own[:, None, :], 'ord', axis=1, tiled=True)  27.3 us
    cos x1, other arithmetic, fourier_table(): return jnp.concatenate([jnp.cos(angle_value), jnp.sin(angle_value)], axis=1)  8.9 us
  transfers between devices with their start and end apart: 4, of which 3 were waited for; matrix products, arithmetic and copies ran while one was open for 6% of the time, Pallas kernels for 0%

commit v1 on v0

--- a/solution.py
+++ b/solution.py
@@ -5,6 +5,15 @@
 from jax.sharding import PartitionSpec as P
 
 LMAX = 2190
+
+
+def connect_the_block(a0, group_axis):
+    nd = lax.axis_size(group_axis)
+    crops = [nd if h == 1 else 1 for h in range(a0.ndim)]
+    new = lax.all_to_all(
+        jnp.tile(a0, crops), tiled=True, split_axis=1, concat_axis=1, axis_name=group_axis
+    )
+    return new
 
 
 def window_flags(first_degree, order_now, half_count):
@@ -77,7 +86,7 @@
     right_cos = products[0] + sign_own * products[2]
     right_sin = products[1] + sign_own * products[3]
     right_side = jnp.stack([right_cos, right_sin], axis=0)[None, None, :, None, :]
-    parity_pair = lax.all_gather(masked_own[:, None, :], "ord", axis=1, tiled=True)
+    parity_pair = connect_the_block(masked_own[:, None, :], "ord")
     plus_weight = (row_weight[0] + row_weight[1])[:, None, None]
     minus_weight = (row_weight[0] - row_weight[1])[:, None, None]
     plus_panel = (parity_pair.astype(jnp.float32) * plus_weight).astype(jnp.bfloat16)

time: 387 us -> 376 us (0.972)
  blocking collectives: 38.5 us -> 16.2 us
  starting transfers between devices: 7.58 us -> 26.8 us
  waiting for transfers between devices: 287 us -> 280 us
    unnamed x4 -> x3, waiting for transfers between devices: 213 us -> 261 us
    all_to_all x1, waiting for transfers between devices: 46.8 us -> 0.01 us  [shards(): lax.all_to_all(panel, 'lat', split_axis=1, concat_axis=2, tiled=True)]
    all_gather x1 -> x0, waiting for transfers between devices: 27.3 us -> none  [shards(): lax.all_gather(masked_own[:, None, :], 'ord', axis=1, tiled=True)]
    all_to_all x1, blocking collectives: 38.5 us -> 16.2 us  [connect_the_block(): lax.all_to_all(jnp.tile(a0, crops), tiled=True, split_axis=1, concat_axis...]
    all_to_all x0 -> x1, waiting for transfers between devices: none -> 19.4 us  [shards(): lax.all_to_all(buffer, 'lat', split_axis=1, concat_axis=1, tiled=True)]
    all_to_all x0 -> x1, starting transfers between devices: none -> 19.3 us  [shards(): lax.all_to_all(buffer, 'lat', split_axis=1, concat_axis=1, tiled=True)]
  transfers between devices with their start and end apart: 4 -> 4, of which waited for: 3 -> 2; matrix products, arithmetic and copies ran while one was open for 6% -> 5% of each run, Pallas kernels for 0% -> 0%
where the time goes in v1:
time: 376 us; the launch traced here: 375 us
  waiting for transfers between devices  280 us (74%)
  starting transfers between devices  26.8 us (7%)
  between operations  16.4 us (4%)
  blocking collectives  16.2 us (4%)
  local copies, waits for them, and re-layouts  15 us (4%)
  other arithmetic  12.9 us (3%)
  matrix products  8.12 us (2%)
    unnamed x3, waiting for transfers between devices  261 us
    all_to_all x1, waiting for transfers between devices, shards(): lax.all_to_all(buffer, 'lat', split_axis=1, concat_axis=1, tiled=True)  19.4 us
    all_to_all x1, starting transfers between devices, shards(): lax.all_to_all(buffer, 'lat', split_axis=1, concat_axis=1, tiled=True)  19.3 us
    all_to_all x1, blocking collectives, connect_the_block(): lax.all_to_all(jnp.tile(a0, crops), tiled=True, split_axis=1, concat_axis...  16.2 us
    cos x1, other arithmetic, fourier_table(): return jnp.concatenate([jnp.cos(angle_value), jnp.sin(angle_value)], axis=1)  8.9 us
  transfers between devices with their start and end apart: 4, of which 2 were waited for; matrix products, arithmetic and copies ran while one was open for 5% of the time, Pallas kernels for 0%

profile of v1, /device:TPU:1, one launch (start us, length us, event | category | flops | bytes accessed | tf_op | source)
XLA Modules:
  0.0 375.4 jit_solution(11321519771747188495)
XLA Ops:
  8.0 0.0 copy-start
  8.0 0.0 copy-start.1
  8.0 0.9 convert_reduce_fusion
  9.0 0.7 compare_select_fusion.2
  9.7 1.0 copy.57
  10.7 0.1 reshape.230
  10.8 0.1 copy.59
  10.9 0.0 copy-start.2
  10.9 1.5 scatter_custom_fusion
  12.4 0.1 reshape.232
  12.5 0.9 copy.60
  13.4 19.3 %all-to-all-start.2 = ((bf16[4,64,2,256]{3,2,0,1:T(2,128)(2,1)}), bf16[4,64,2,256]{3,2,0,1:T(2,128)(2,1)S(1)}, u32[]{:S(2)}, u32[]{:S(2)}) async-start(bf16[4,64,2,256]{3,2,0,1:T(2,128)(2,1)} %copy.60), calls=%async_computation.2 | async-start | bytes 524288 | tf_op jit(solution)/shard_map/all_to_all | solution.py:124
  32.7 0.0 copy-done.1
  32.7 0.1 constant_dynamic-slice_fusion.1
  32.8 19.4 %all-to-all-done.2 = bf16[4,64,2,256]{3,2,0,1:T(2,128)(2,1)S(1)} async-done(((bf16[4,64,2,256]{3,2,0,1:T(2,128)(2,1)}), bf16[4,64,2,256]{3,2,0,1:T(2,128)(2,1)S(1)}, u32[]{:S(2)}, u32[]{:S(2)}) %all-to-all-start.2) | async-done | bytes 262176 | tf_op jit(solution)/shard_map/all_to_all | solution.py:124
  52.2 7.0 %all-to-all-start = ((bf16[1,64,16,1,640]{4,2,3,0,1:T(8,128)(2,1)}), bf16[1,64,16,1,640]{4,2,3,0,1:T(8,128)(2,1)S(1)}, u32[]{:S(2)}, u32[]{:S(2)}) async-start(bf16[1,64,16,1,640]{4,2,3,0,1:T(8,128)(2,1)} %bitcast), calls=%async_computation | async-start | bytes 2621440 | tf_op jit(solution)/shard_map/all_to_all | solution.py:84
  59.2 0.2 all-reduce.4.cloned.1.call-start
  59.5 0.0 copy-done.2
  59.5 8.9 %fusion.16 = (f32[4320,64]{1,0:T(8,128)S(1)}, f32[4320,64]{1,0:T(8,128)S(1)}) fusion(s32[64]{0:T(128)S(1)} %bitcast.96), kind=kLoop, calls=%fused_computation.21 | loop fusion | flops 2488320 | bytes 2212096 | tf_op jit(solution)/shard_map/cos | solution.py:34
  68.4 0.0 copy-done
  68.4 1.2 fusion.25
  69.6 0.1 fusion.33
  69.7 0.1 slice_bitcast_fusion.3
  69.8 0.1 copy.67
  69.9 2.5 fusion.20
  72.4 0.0 all-reduce.4.cloned.1.call-update
  72.4 0.3 reduce-scatter.2.cloned.1.call-start
  72.7 0.2 copy.61
  72.9 0.2 reshape_reshape.3
  73.1 0.1 reshape.233
  73.2 0.2 copy.63
  73.4 0.3 fusion.44
  73.6 1.0 copy.64
  74.7 0.0 reduce-scatter.2.cloned.1.call-update
  74.7 0.6 constant_dynamic-slice_fusion
  76.0 0.7 compare_select_fusion
  76.7 1.3 dynamic-slice.3
  78.0 260.6 %all-reduce.4.cloned.1.call-done = f32[64,4,640]{2,1,0:T(4,128)} async-done(((f32[64,4,640]{2,1,0:T(4,128)}), f32[64,4,640]{2,1,0:T(4,128)}) %all-reduce.4.cloned.1.call-update) | async-done | bytes 655376
  338.5 1.4 fusion.29
  339.9 0.6 copy.69
  340.5 0.0 reduce-scatter.2.cloned.1.call-done
  340.5 1.0 copy.65
  341.5 0.1 copy.66
  341.7 0.0 all-to-all-done
  341.7 0.7 copy.55
  342.3 0.2 broadcast_multiply_fusion
  342.5 0.7 copy.56
  343.2 0.2 tile.2
  343.4 16.2 %all_to_all.19 = bf16[1024,2,640]{2,0,1:T(8,128)(2,1)S(1)} all-to-all(bf16[1024,2,640]{2,0,1:T(8,128)(2,1)S(1)} %tile.2), channel_id=1, replica_groups=mesh['lat'=64,'ord'=2,'orb'=4] {'ord'}, dimensions={1} | all-to-all | bytes 5242880 | tf_op jit(solution)/shard_map/all_to_all | solution.py:13
  359.6 2.0 fusion.2
  361.7 2.1 add_bitcast_fusion
  363.8 4.2 %copy.68 = f32[1,1,1,640,2,640]{5,4,3,2,1,0:T(2,128)} copy(f32[1,1,1,640,2,640]{5,3,4,2,1,0:T(8,128)S(1)} %add_bitcast_fusion) | data formatting | bytes 6553600
  (11 shorter events, 0.1 us)
Async XLA Ops:
  8.0 60.4 %copy-start = (bf16[2,16,4320]{2,1,0:T(8,128)(2,1)S(1)}, bf16[2,16,4320]{2,1,0:T(8,128)(2,1)}, u32[]{:S(2)}) copy-start(bf16[2,16,4320]{2,1,0:T(8,128)(2,1)} %param.7) | copy-start | bytes 829444
  8.0 24.7 %copy-start.1 = (f32[2,1024]{1,0:T(2,128)S(1)}, f32[2,1024]{1,0:T(2,128)}, u32[]{:S(2)}) copy-start(f32[2,1024]{1,0:T(2,128)} %param.8) | copy-start | bytes 24580
  10.9 48.6 %copy-start.2 = (s32[1,64]{1,0:T(1,128)S(1)}, s32[1,64]{1,0:T(1,128)}, u32[]{:S(2)}) copy-start(s32[1,64]{1,0:T(1,128)} %param.10) | copy-start | bytes 772
  13.4 38.8 %all-to-all-start.2 = ((bf16[4,64,2,256]{3,2,0,1:T(2,128)(2,1)}), bf16[4,64,2,256]{3,2,0,1:T(2,128)(2,1)S(1)}, u32[]{:S(2)}, u32[]{:S(2)}) async-start(bf16[4,64,2,256]{3,2,0,1:T(2,128)(2,1)} %copy.60), calls=%async_computation.2 | async-start | bytes 524288 | tf_op jit(solution)/shard_map/all_to_all | solution.py:124
  52.2 289.5 %all-to-all-start = ((bf16[1,64,16,1,640]{4,2,3,0,1:T(8,128)(2,1)}), bf16[1,64,16,1,640]{4,2,3,0,1:T(8,128)(2,1)S(1)}, u32[]{:S(2)}, u32[]{:S(2)}) async-start(bf16[1,64,16,1,640]{4,2,3,0,1:T(8,128)(2,1)} %bitcast), calls=%async_computation | async-start | bytes 2621440 | tf_op jit(solution)/shard_map/all_to_all | solution.py:84
  59.2 279.3 %all-reduce.4.cloned.1.call-start = ((), (), s32[]{:S(2)}) async-start(), calls=%async_computation.5 | async-start | bytes 1310720
  72.4 268.1 %reduce-scatter.2.cloned.1.call-start = ((), (), s32[]{:S(2)}) async-start(), calls=%async_computation.4 | async-start | bytes 1179648 | tf_op jit(solution)/shard_map/reduce_scatter | solution.py:126
Sparse Core Ops, SparseCore 0:
  72.5 265.9 all-reduce.3
Sparse Core Ops, SparseCore 1:
  76.3 44.1 reduce-scatter.1
